TPU v7x, 32 devices: a whole 2x2x4 slice. The times are simulated.
32 devices in a mesh: dp: 4 (over y, x), seg: 8 (over z, core).
Axes of the slice: x: 2, y: 2, z: 4, core: 2. Of those that a mesh axis runs over, the one named last changes fastest.
Arguments:
- inputs: bfloat16 [4, 4096, 768], P('dp', 'seg'), may hold values from -6 to 6
- doc_ids: int32 [4, 32], P('dp'), may hold values from 0 to 7, never falling along the last dimension, each value on 1 to 16 neighbouring positions
- cotangent: bfloat16 [4, 4096, 768], P('dp', 'seg'), may hold values from -6 to 6
- query_weight: bfloat16 [2, 768, 768], P(None, 'dp'), may hold values from -0.21875 to 0.21875
- query_bias: bfloat16 [2, 768], replicated, may hold values from -3 to 3
- key_weight: bfloat16 [2, 768, 768], P(None, 'dp'), may hold values from -0.21875 to 0.21875
- value_weight: bfloat16 [2, 768, 768], P(None, 'dp'), may hold values from -0.21875 to 0.21875
- value_bias: bfloat16 [2, 768], replicated, may hold values from -3 to 3
- out_weight: bfloat16 [2, 768, 768], P(None, 'dp'), may hold values from -1.75 to 1.75
- out_bias: bfloat16 [2, 768], replicated, may hold values from -3 to 3
- first_gain: bfloat16 [2, 768], replicated, may hold values from 0.5 to 1.5
- first_shift: bfloat16 [2, 768], replicated, may hold values from -2 to 2
- inner_weight: bfloat16 [2, 768, 3072], P(None, 'dp'), may hold values from -0.21875 to 0.21875
- inner_bias: bfloat16 [2, 3072], replicated, may hold values from -3 to 3
- outer_weight: bfloat16 [2, 3072, 768], P(None, 'dp'), may hold values from -0.109375 to 0.109375
- outer_bias: bfloat16 [2, 768], replicated, may hold values from -3 to 3
- second_gain: bfloat16 [2, 768], replicated, may hold values from 0.5 to 1.5
- second_shift: bfloat16 [2, 768], replicated, may hold values from -2 to 2
- segment_embed: bfloat16 [32, 768], replicated, may hold values from -3 to 3
Outputs:
- output: bfloat16 [4, 4096, 768], P('dp', 'seg')
- input_grad: bfloat16 [4, 4096, 768], P('dp', 'seg')
- grad_query_weight: float32 [2, 768, 768], P(None, 'dp')
- grad_query_bias: float32 [2, 768], P(None, 'dp')
- grad_key_weight: float32 [2, 768, 768], P(None, 'dp')
- grad_value_weight: float32 [2, 768, 768], P(None, 'dp')
- grad_value_bias: float32 [2, 768], P(None, 'dp')
- grad_out_weight: float32 [2, 768, 768], P(None, 'dp')
- grad_out_bias: float32 [2, 768], P(None, 'dp')
- grad_first_gain: float32 [2, 768], P(None, 'dp')
- grad_first_shift: float32 [2, 768], P(None, 'dp')
- grad_inner_weight: float32 [2, 768, 3072], P(None, 'dp')
- grad_inner_bias: float32 [2, 3072], P(None, 'dp')
- grad_outer_weight: float32 [2, 3072, 768], P(None, 'dp')
- grad_outer_bias: float32 [2, 768], P(None, 'dp')
- grad_second_gain: float32 [2, 768], P(None, 'dp')
- grad_second_shift: float32 [2, 768], P(None, 'dp')
- grad_segment_embed: float32 [32, 768], P(None, 'dp')
Inputs may be any that keep to these rules, and one draw needn't show every extreme that they name: `doc_ids`: along each row document numbers never fall; each document covers one to half of 32 consecutive segments, and some document of each row covers exactly half of 32.
All inputs are finite; a program needn't handle non-finite values.
Results may differ from a plain program's by a relative error of at most 0.02.
Values may be sent and summed in bfloat16 or wider, within the bound.
A program may use at most 256 MiB of HBM per device.

v0:
```python
import jax
import jax.numpy as jnp
from jax import lax
from jax.sharding import PartitionSpec as P

HEADS = 12
HEAD_DIM = 64
SEG_LEN = 128
epsilon = 1e-05


def normalize(values, gain, shift):
    centred = values - jnp.mean(values, axis=-1, keepdims=True)
    spread = jnp.mean(centred * centred, axis=-1, keepdims=True)
    return centred * lax.rsqrt(spread + epsilon) * gain + shift


def gelu_exact(values):
    return jax.nn.gelu(values, approximate=False)


def project(values, weight):
    return jnp.einsum("gnd,de->gne", values, weight, preferred_element_type=jnp.float32)


def back_project(values, weight):
    return jnp.einsum("gne,de->gnd", values, weight, preferred_element_type=jnp.float32)


def weight_grad(source, grads):
    return jnp.einsum("gnd,gne->de", source, grads, preferred_element_type=jnp.float32)


def row_total(values):
    return jnp.sum(values.astype(jnp.float32), axis=(0, 1))


def keep_pair(first_part, second_part):
    return (first_part, second_part)


def forward_layer(params, source, allowed, spread_keys):
    (
        query_weight,
        query_bias,
        key_weight,
        value_weight,
        value_bias,
        out_weight,
        out_bias,
        first_gain,
        first_shift,
        inner_weight,
        inner_bias,
        outer_weight,
        outer_bias,
        second_gain,
        second_shift,
    ) = params
    groups, length, width = source.shape
    queries = (project(source, query_weight) + query_bias.astype(jnp.float32)).astype(jnp.bfloat16)
    key_rows = project(source, key_weight).astype(jnp.bfloat16)
    value_rows = (project(source, value_weight) + value_bias.astype(jnp.float32)).astype(
        jnp.bfloat16
    )
    key_all, value_all = spread_keys(key_rows, value_rows)
    key_length = key_all.shape[1]
    query_heads = queries.reshape(groups, length, HEADS, HEAD_DIM)
    key_heads = key_all.reshape(groups, key_length, HEADS, HEAD_DIM)
    value_heads = value_all.reshape(groups, key_length, HEADS, HEAD_DIM)
    scores = (
        jnp.einsum("gqhe,gkhe->ghqk", query_heads, key_heads, preferred_element_type=jnp.float32)
        * 0.125
    )
    if allowed is not None:
        scores = jnp.where(allowed[:, None], scores, -1e30)
    attend = jax.nn.softmax(scores, axis=-1)
    attend_low = attend.astype(jnp.bfloat16)
    mixed = jnp.einsum(
        "ghqk,gkhe->gqhe", attend_low, value_heads, preferred_element_type=jnp.float32
    )
    mixed = mixed.astype(jnp.bfloat16).reshape(groups, length, width)
    branch = project(mixed, out_weight) + out_bias.astype(jnp.float32)
    hidden, first_pull = jax.vjp(
        normalize,
        source.astype(jnp.float32) + branch,
        first_gain.astype(jnp.float32),
        first_shift.astype(jnp.float32),
    )
    hidden_low = hidden.astype(jnp.bfloat16)
    inner = project(hidden_low, inner_weight) + inner_bias.astype(jnp.float32)
    active, gelu_pull = jax.vjp(gelu_exact, inner)
    active_low = active.astype(jnp.bfloat16)
    outer = project(active_low, outer_weight) + outer_bias.astype(jnp.float32)
    result, second_pull = jax.vjp(
        normalize, hidden + outer, second_gain.astype(jnp.float32), second_shift.astype(jnp.float32)
    )
    stored = (
        source,
        query_heads,
        key_heads,
        value_heads,
        attend,
        attend_low,
        mixed,
        first_pull,
        hidden_low,
        gelu_pull,
        active_low,
        second_pull,
    )
    return (result, stored)


def backward_layer(params, stored, grad_result, collect_keys):
    (
        query_weight,
        query_bias,
        key_weight,
        value_weight,
        value_bias,
        out_weight,
        out_bias,
        first_gain,
        first_shift,
        inner_weight,
        inner_bias,
        outer_weight,
        outer_bias,
        second_gain,
        second_shift,
    ) = params
    (
        source,
        query_heads,
        key_heads,
        value_heads,
        attend,
        attend_low,
        mixed,
        first_pull,
        hidden_low,
        gelu_pull,
        active_low,
        second_pull,
    ) = stored
    groups, length, width = source.shape
    key_length = key_heads.shape[1]
    grad_second_sum, grad_second_gain, grad_second_shift = second_pull(grad_result)
    grad_outer = grad_second_sum.astype(jnp.bfloat16)
    grad_outer_bias = row_total(grad_outer)
    grad_outer_weight = weight_grad(active_low, grad_outer)
    grad_active = back_project(grad_outer, outer_weight).astype(jnp.bfloat16)
    (grad_inner,) = gelu_pull(grad_active.astype(jnp.float32))
    grad_inner_low = grad_inner.astype(jnp.bfloat16)
    grad_inner_bias = row_total(grad_inner_low)
    grad_inner_weight = weight_grad(hidden_low, grad_inner_low)
    grad_hidden = grad_second_sum + back_project(grad_inner_low, inner_weight)
    grad_first_sum, grad_first_gain, grad_first_shift = first_pull(grad_hidden)
    grad_branch = grad_first_sum.astype(jnp.bfloat16)
    grad_out_bias = row_total(grad_branch)
    grad_out_weight = weight_grad(mixed, grad_branch)
    grad_mixed = back_project(grad_branch, out_weight).astype(jnp.bfloat16)
    grad_mixed = grad_mixed.reshape(groups, length, HEADS, HEAD_DIM)
    grad_attend = jnp.einsum(
        "gqhe,gkhe->ghqk", grad_mixed, value_heads, preferred_element_type=jnp.float32
    )
    grad_attend = grad_attend.astype(jnp.bfloat16).astype(jnp.float32)
    grad_value = jnp.einsum(
        "ghqk,gqhe->gkhe", attend_low, grad_mixed, preferred_element_type=jnp.float32
    )
    grad_value = grad_value.reshape(groups, key_length, width)
    grad_scores = attend * (grad_attend - jnp.sum(attend * grad_attend, axis=-1, keepdims=True))
    grad_scores = grad_scores.astype(jnp.bfloat16)
    grad_query = (
        jnp.einsum("ghqk,gkhe->gqhe", grad_scores, key_heads, preferred_element_type=jnp.float32)
        * 0.125
    )
    grad_query = grad_query.astype(jnp.bfloat16).reshape(groups, length, width)
    grad_key = (
        jnp.einsum("ghqk,gqhe->gkhe", grad_scores, query_heads, preferred_element_type=jnp.float32)
        * 0.125
    )
    grad_key = grad_key.reshape(groups, key_length, width)
    grad_key, grad_value = collect_keys(grad_key, grad_value)
    grad_key = grad_key.astype(jnp.bfloat16)
    grad_value = grad_value.astype(jnp.bfloat16)
    grad_source = (
        grad_first_sum
        + back_project(grad_query, query_weight)
        + back_project(grad_key, key_weight)
        + back_project(grad_value, value_weight)
    )
    gradients = (
        weight_grad(source, grad_query),
        row_total(grad_query),
        weight_grad(source, grad_key),
        weight_grad(source, grad_value),
        row_total(grad_value),
        grad_out_weight,
        grad_out_bias,
        grad_first_gain,
        grad_first_shift,
        grad_inner_weight,
        grad_inner_bias,
        grad_outer_weight,
        grad_outer_bias,
        grad_second_gain,
        grad_second_shift,
    )
    return (grad_source, gradients)


def shards(
    inputs,
    doc_ids,
    cotangent,
    query_weight,
    query_bias,
    key_weight,
    value_weight,
    value_bias,
    out_weight,
    out_bias,
    first_gain,
    first_shift,
    inner_weight,
    inner_bias,
    outer_weight,
    outer_bias,
    second_gain,
    second_shift,
    segment_embed,
):
    seg_count = lax.axis_size("seg")
    seg_index = lax.axis_index("seg")
    group_rows, local_length, width = inputs.shape
    seg_local = local_length // SEG_LEN
    query_full, key_full, value_full, out_full, inner_full, outer_full = (
        lax.all_gather(query_weight, "dp", axis=1, tiled=True),
        lax.all_gather(key_weight, "dp", axis=1, tiled=True),
        lax.all_gather(value_weight, "dp", axis=1, tiled=True),
        lax.all_gather(out_weight, "dp", axis=1, tiled=True),
        lax.all_gather(inner_weight, "dp", axis=1, tiled=True),
        lax.all_gather(outer_weight, "dp", axis=1, tiled=True),
    )
    stacked = (
        query_full,
        query_bias,
        key_full,
        value_full,
        value_bias,
        out_full,
        out_bias,
        first_gain,
        first_shift,
        inner_full,
        inner_bias,
        outer_full,
        outer_bias,
        second_gain,
        second_shift,
    )
    first_params = tuple((weight[0] for weight in stacked))
    cross_params = tuple((weight[1] for weight in stacked))
    pieces = inputs.reshape(group_rows * seg_local, SEG_LEN, width)
    segment_out, segment_stored = forward_layer(first_params, pieces, None, keep_pair)
    segment_grid = segment_out.reshape(group_rows, seg_local, SEG_LEN, width)
    position = lax.dynamic_slice_in_dim(segment_embed, seg_index * seg_local, seg_local, 0).astype(
        jnp.float32
    )
    heads_in = (segment_grid[:, :, 0, :] + position).astype(jnp.bfloat16)
    row_input = lax.all_gather(heads_in, "seg", axis=1, tiled=True)
    allowed = doc_ids[:, :, None] == doc_ids[:, None, :]
    cross_out, cross_stored = forward_layer(cross_params, row_input, allowed, keep_pair)
    returned = lax.dynamic_slice_in_dim(cross_out, seg_index * seg_local, seg_local, 1).astype(
        jnp.bfloat16
    )
    output = jnp.concatenate(
        [returned[:, :, None, :], segment_grid[:, :, 1:, :].astype(jnp.bfloat16)], axis=2
    )
    output = output.reshape(group_rows, local_length, width)
    cot_grid = cotangent.reshape(group_rows, seg_local, SEG_LEN, width)
    cot_heads = cot_grid[:, :, 0, :]
    grad_cross = lax.all_gather(cot_heads, "seg", axis=1, tiled=True)
    grad_row_input, cross_grads = backward_layer(
        cross_params, cross_stored, grad_cross.astype(jnp.float32), keep_pair
    )
    grad_row_low = grad_row_input.astype(jnp.bfloat16)
    factor = 1.0 / seg_count
    embed_grad = jnp.sum(grad_row_low.astype(jnp.float32), axis=0) * factor
    cross_grads = tuple((part * factor for part in cross_grads))
    grad_heads = lax.dynamic_slice_in_dim(grad_row_low, seg_index * seg_local, seg_local, 1)
    grad_grid = jnp.concatenate(
        [grad_heads[:, :, None, :].astype(jnp.float32), cot_grid[:, :, 1:, :].astype(jnp.float32)],
        axis=2,
    )
    grad_grid = grad_grid.reshape(group_rows * seg_local, SEG_LEN, width)
    grad_pieces, segment_grads = backward_layer(first_params, segment_stored, grad_grid, keep_pair)
    input_grad = grad_pieces.astype(jnp.bfloat16).reshape(group_rows, local_length, width)
    shares = (
        lax.psum_scatter(segment_grads[0], "dp", scatter_dimension=0, tiled=True),
        lax.psum_scatter(segment_grads[1], "dp", scatter_dimension=0, tiled=True),
        lax.psum_scatter(segment_grads[2], "dp", scatter_dimension=0, tiled=True),
        lax.psum_scatter(segment_grads[3], "dp", scatter_dimension=0, tiled=True),
        lax.psum_scatter(segment_grads[4], "dp", scatter_dimension=0, tiled=True),
        lax.psum_scatter(segment_grads[5], "dp", scatter_dimension=0, tiled=True),
        lax.psum_scatter(segment_grads[6], "dp", scatter_dimension=0, tiled=True),
        lax.psum_scatter(segment_grads[7], "dp", scatter_dimension=0, tiled=True),
        lax.psum_scatter(segment_grads[8], "dp", scatter_dimension=0, tiled=True),
        lax.psum_scatter(segment_grads[9], "dp", scatter_dimension=0, tiled=True),
        lax.psum_scatter(segment_grads[10], "dp", scatter_dimension=0, tiled=True),
        lax.psum_scatter(segment_grads[11], "dp", scatter_dimension=0, tiled=True),
        lax.psum_scatter(segment_grads[12], "dp", scatter_dimension=0, tiled=True),
        lax.psum_scatter(segment_grads[13], "dp", scatter_dimension=0, tiled=True),
        lax.psum_scatter(segment_grads[14], "dp", scatter_dimension=0, tiled=True),
        lax.psum_scatter(cross_grads[0], "dp", scatter_dimension=0, tiled=True),
        lax.psum_scatter(cross_grads[1], "dp", scatter_dimension=0, tiled=True),
        lax.psum_scatter(cross_grads[2], "dp", scatter_dimension=0, tiled=True),
        lax.psum_scatter(cross_grads[3], "dp", scatter_dimension=0, tiled=True),
        lax.psum_scatter(cross_grads[4], "dp", scatter_dimension=0, tiled=True),
        lax.psum_scatter(cross_grads[5], "dp", scatter_dimension=0, tiled=True),
        lax.psum_scatter(cross_grads[6], "dp", scatter_dimension=0, tiled=True),
        lax.psum_scatter(cross_grads[7], "dp", scatter_dimension=0, tiled=True),
        lax.psum_scatter(cross_grads[8], "dp", scatter_dimension=0, tiled=True),
        lax.psum_scatter(cross_grads[9], "dp", scatter_dimension=0, tiled=True),
        lax.psum_scatter(cross_grads[10], "dp", scatter_dimension=0, tiled=True),
        lax.psum_scatter(cross_grads[11], "dp", scatter_dimension=0, tiled=True),
        lax.psum_scatter(cross_grads[12], "dp", scatter_dimension=0, tiled=True),
        lax.psum_scatter(cross_grads[13], "dp", scatter_dimension=0, tiled=True),
        lax.psum_scatter(cross_grads[14], "dp", scatter_dimension=0, tiled=True),
        lax.psum_scatter(embed_grad, "dp", scatter_dimension=1, tiled=True),
    )
    summed = lax.psum(
        (
            shares[0],
            shares[1],
            shares[2],
            shares[3],
            shares[4],
            shares[5],
            shares[6],
            shares[7],
            shares[8],
            shares[9],
            shares[10],
            shares[11],
            shares[12],
            shares[13],
            shares[14],
            shares[15],
            shares[16],
            shares[17],
            shares[18],
            shares[19],
            shares[20],
            shares[21],
            shares[22],
            shares[23],
            shares[24],
            shares[25],
            shares[26],
            shares[27],
            shares[28],
            shares[29],
            shares[30],
        ),
        "seg",
    )
    totals = tuple((jnp.stack([summed[index], summed[index + 15]]) for index in range(15)))
    totals = totals + (summed[30],)
    return (output, input_grad) + tuple(totals)


def solution(mesh):
    placed = (
        P("dp", "seg", None),
        P("dp", None),
        P("dp", "seg", None),
        P(None, "dp", None),
        P(),
        P(None, "dp", None),
        P(None, "dp", None),
        P(),
        P(None, "dp", None),
        P(),
        P(),
        P(),
        P(None, "dp", None),
        P(),
        P(None, "dp", None),
        P(),
        P(),
        P(),
        P(),
    )
    return jax.shard_map(
        shards,
        mesh=mesh,
        in_specs=placed,
        out_specs=(
            P("dp", "seg", None),
            P("dp", "seg", None),
            P(None, "dp", None),
            P(None, "dp"),
            P(None, "dp", None),
            P(None, "dp", None),
            P(None, "dp"),
            P(None, "dp", None),
            P(None, "dp"),
            P(None, "dp"),
            P(None, "dp"),
            P(None, "dp", None),
            P(None, "dp"),
            P(None, "dp", None),
            P(None, "dp"),
            P(None, "dp"),
            P(None, "dp"),
            P(None, "dp"),
        ),
        check_vma=False,
    )
```

profile of v0, /device:TPU:0, one launch (start us, length us, event | category | flops | bytes accessed | tf_op | source)
XLA Modules:
  0.0 1615.4 jit_solution(5747079479511893777)
XLA Ops:
  11.4 15.6 all-gather.1
  32.1 17.8 %all-gather.10.cloned.1.call-done = bf16[2,768,768]{2,1,0:T(8,128)(2,1)} async-done(((bf16[2,192,768]{2,1,0:T(8,128)(2,1)}), bf16[2,768,768]{2,1,0:T(8,128)(2,1)}) %all-gather.10.cloned.1.call-update) | async-done | bytes 2359312 | tf_op jit(solution)/shard_map/all_gather | solution.py:242
  53.2 36.0 %all-gather.12.cloned.1.call-done = bf16[2,768,768]{2,1,0:T(8,128)(2,1)} async-done(((bf16[2,192,768]{2,1,0:T(8,128)(2,1)}), bf16[2,768,768]{2,1,0:T(8,128)(2,1)}) %all-gather.12.cloned.1.call-update) | async-done | bytes 2359312 | tf_op jit(solution)/shard_map/all_gather | solution.py:240
  91.6 36.8 %all-gather.14.cloned.1.call-done = bf16[2,768,768]{2,1,0:T(8,128)(2,1)} async-done(((bf16[2,192,768]{2,1,0:T(8,128)(2,1)}), bf16[2,768,768]{2,1,0:T(8,128)(2,1)}) %all-gather.14.cloned.1.call-update) | async-done | bytes 2359312 | tf_op jit(solution)/shard_map/all_gather | solution.py:241
  136.5 31.0 %all-gather.16.cloned.1.call-done = bf16[2,768,768]{2,1,0:T(8,128)(2,1)} async-done(((bf16[2,192,768]{2,1,0:T(8,128)(2,1)}), bf16[2,768,768]{2,1,0:T(8,128)(2,1)}) %all-gather.16.cloned.1.call-update) | async-done | bytes 2359312 | tf_op jit(solution)/shard_map/all_gather | solution.py:243
  170.0 95.4 %all-gather.18.cloned.1.call-done = bf16[2,768,3072]{2,1,0:T(8,128)(2,1)} async-done(((bf16[2,192,3072]{2,1,0:T(8,128)(2,1)}), bf16[2,768,3072]{2,1,0:T(8,128)(2,1)}) %all-gather.18.cloned.1.call-update) | async-done | bytes 9437200 | tf_op jit(solution)/shard_map/all_gather | solution.py:244
  275.6 15.7 multiply_convert_fusion
  291.3 72.1 %all-gather.20.cloned.1.call-done = bf16[2,3072,768]{2,1,0:T(8,128)(2,1)} async-done(((bf16[2,768,768]{2,1,0:T(8,128)(2,1)}), bf16[2,3072,768]{2,1,0:T(8,128)(2,1)}) %all-gather.20.cloned.1.call-update) | async-done | bytes 9437200 | tf_op jit(solution)/shard_map/all_gather | solution.py:245
  372.5 14.1 all-gather.2
  439.2 9.9 multiply_reduce_fusion.1
  557.5 38.3 %reduce-scatter.44.cloned.1.call-done = f32[192,768]{1,0:T(8,128)} async-done(((f32[768,768]{1,0:T(8,128)}), f32[192,768]{1,0:T(8,128)}) %reduce-scatter.44.cloned.1.call-update) | async-done | bytes 589840
  598.0 38.1 %reduce-scatter.52.cloned.1.call-done = f32[192,768]{1,0:T(8,128)} async-done(((f32[768,768]{1,0:T(8,128)}), f32[192,768]{1,0:T(8,128)}) %reduce-scatter.52.cloned.1.call-update) | async-done | bytes 589840
  638.3 38.2 %reduce-scatter.54.cloned.1.call-done = f32[192,768]{1,0:T(8,128)} async-done(((f32[768,768]{1,0:T(8,128)}), f32[192,768]{1,0:T(8,128)}) %reduce-scatter.54.cloned.1.call-update) | async-done | bytes 589840
  678.8 38.1 %reduce-scatter.50.cloned.1.call-done = f32[192,768]{1,0:T(8,128)} async-done(((f32[768,768]{1,0:T(8,128)}), f32[192,768]{1,0:T(8,128)}) %reduce-scatter.50.cloned.1.call-update) | async-done | bytes 589840
  719.1 38.8 %reduce-scatter.42.cloned.1.call-done = f32[192,768]{1,0:T(8,128)} async-done(((f32[768,768]{1,0:T(8,128)}), f32[192,768]{1,0:T(8,128)}) %reduce-scatter.42.cloned.1.call-update) | async-done | bytes 589840
  760.1 38.1 %reduce-scatter.46.cloned.1.call-done = f32[192,768]{1,0:T(8,128)} async-done(((f32[768,768]{1,0:T(8,128)}), f32[192,768]{1,0:T(8,128)}) %reduce-scatter.46.cloned.1.call-update) | async-done | bytes 589840
  800.4 95.7 %reduce-scatter.32.cloned.1.call-done = f32[192,3072]{1,0:T(8,128)} async-done(((f32[768,3072]{1,0:T(8,128)}), f32[192,3072]{1,0:T(8,128)}) %reduce-scatter.32.cloned.1.call-update) | async-done | bytes 2359312 | tf_op jit(solution)/shard_map/reduce_scatter | solution.py:311
  896.1 97.9 %reduce-scatter.36.cloned.1.call-done = f32[768,768]{1,0:T(8,128)} async-done(((f32[3072,768]{1,0:T(8,128)}), f32[768,768]{1,0:T(8,128)}) %reduce-scatter.36.cloned.1.call-update) | async-done | bytes 2359312 | tf_op jit(solution)/shard_map/reduce_scatter | solution.py:313
  994.0 97.9 %reduce-scatter.38.cloned.1.call-done = f32[768,768]{1,0:T(8,128)} async-done(((f32[3072,768]{1,0:T(8,128)}), f32[768,768]{1,0:T(8,128)}) %reduce-scatter.38.cloned.1.call-update) | async-done | bytes 2359312 | tf_op jit(solution)/shard_map/reduce_scatter | solution.py:328
  1091.9 97.9 %reduce-scatter.34.cloned.1.call-done = f32[192,3072]{1,0:T(8,128)} async-done(((f32[768,3072]{1,0:T(8,128)}), f32[192,3072]{1,0:T(8,128)}) %reduce-scatter.34.cloned.1.call-update) | async-done | bytes 2359312 | tf_op jit(solution)/shard_map/reduce_scatter | solution.py:326
  1200.1 44.1 %all-reduce.26.cloned.1.call-done = (f32[768]{0:T(1024)}, f32[768]{0:T(1024)}, f32[768]{0:T(1024)}, f32[768]{0:T(1024)}, f32[768]{0:T(1024)}, /*index=5*/f32[768...) async-done(((f32[768]{0:T(1024)}, f32[768]{0:T(1024)}, ...) | async-done | bytes 73744
  1257.8 13.8 reduce-scatter.56.cloned.1.call-done
  1272.6 30.8 %all-reduce.18 = (f32[1,192]{1,0:T(1,128)S(1)}, f32[1,192]{1,0:T(1,128)S(1)}, f32[1,192]{1,0:T(1,128)S(1)}, f32[1,192]{1,0:T(1,128)S(1)}, f32[1,192]{1,0:T(1,128...) all-reduce(f32[1,192]{1,0:T(1,128)S(1)} %bitcast.354, ...), channel_id=1, replica_groups=mesh['dp'=4,'seg'=8] {'seg'}, use_global_device_ids=true, to_apply=%region_31.32 | all-reduce | flops 10752 | bytes 86016 | tf_op jit(solution)/shard_map/psum | solution.py:334
  1308.7 282.4 %all-reduce.24.cloned.1.call-done = (f32[1,192,768]{1,2,0:T(8,128)}, f32[1,192,768]{1,2,0:T(8,128)}, f32[1,192,768]{1,2,0:T(8,128)}, f32[1,192,768]{1,2,0:T(8,12...) async-done(((f32[1,192,768]{1,2,0:T(8,128)}, ...) | async-done | bytes 14155792 | tf_op jit(solution)/shard_map/psum | solution.py:334
  (458 shorter events, 263.6 us)
Async XLA Ops:
  7.2 42.8 %all-gather.10.cloned.1.call-start = ((), (), s32[]{:S(2)}) async-start(), calls=%async_computation.13 | async-start | bytes 2949120 | tf_op jit(solution)/shard_map/all_gather | solution.py:242
  7.9 81.2 %all-gather.12.cloned.1.call-start = ((), (), s32[]{:S(2)}) async-start(), calls=%async_computation.14 | async-start | bytes 2949120 | tf_op jit(solution)/shard_map/all_gather | solution.py:240
  8.7 119.7 %all-gather.14.cloned.1.call-start = ((), (), s32[]{:S(2)}) async-start(), calls=%async_computation.15 | async-start | bytes 2949120 | tf_op jit(solution)/shard_map/all_gather | solution.py:241
  9.4 158.0 %all-gather.16.cloned.1.call-start = ((), (), s32[]{:S(2)}) async-start(), calls=%async_computation.16 | async-start | bytes 2949120 | tf_op jit(solution)/shard_map/all_gather | solution.py:243
  10.1 255.3 %all-gather.18.cloned.1.call-start = ((), (), s32[]{:S(2)}) async-start(), calls=%async_computation.17 | async-start | bytes 11796480 | tf_op jit(solution)/shard_map/all_gather | solution.py:244
  10.7 352.6 %all-gather.20.cloned.1.call-start = ((), (), s32[]{:S(2)}) async-start(), calls=%async_computation.18 | async-start | bytes 11796480 | tf_op jit(solution)/shard_map/all_gather | solution.py:245
  11.3 538.5 %reduce-scatter.48.cloned.1.call-start = ((), (), s32[]{:S(2)}) async-start(), calls=%async_computation.27 | async-start | bytes 2949120
  28.3 335.1 %copy-start.81 = (f32[768]{0:T(1024)}, f32[768]{0:T(1024)S(1)}, u32[]{:S(2)}) copy-start(f32[768]{0:T(1024)S(1)} %get-tuple-element.91) | copy-start | bytes 9220
  28.9 334.4 %copy-start.96 = (f32[768]{0:T(1024)}, f32[768]{0:T(1024)S(1)}, u32[]{:S(2)}) copy-start(f32[768]{0:T(1024)S(1)} %get-tuple-element.207) | copy-start | bytes 9220
  29.5 340.7 %copy-start.58 = (f32[768]{0:T(1024)}, f32[768]{0:T(1024)S(1)}, u32[]{:S(2)}) copy-start(f32[768]{0:T(1024)S(1)} %get-tuple-element.209) | copy-start | bytes 9220
  477.3 78.0 %reduce-scatter.40.cloned.1.call-start = ((), (), s32[]{:S(2)}) async-start(), calls=%async_computation.23 | async-start | bytes 2949120
  489.2 106.6 %reduce-scatter.44.cloned.1.call-start = ((), (), s32[]{:S(2)}) async-start(), calls=%async_computation.25 | async-start | bytes 2949120
  498.1 138.0 %reduce-scatter.52.cloned.1.call-start = ((), (), s32[]{:S(2)}) async-start(), calls=%async_computation.29 | async-start | bytes 2949120
  501.7 174.9 %reduce-scatter.54.cloned.1.call-start = ((), (), s32[]{:S(2)}) async-start(), calls=%async_computation.30 | async-start | bytes 2949120
  504.6 212.3 %reduce-scatter.50.cloned.1.call-start = ((), (), s32[]{:S(2)}) async-start(), calls=%async_computation.28 | async-start | bytes 2949120
  506.6 251.3 %reduce-scatter.42.cloned.1.call-start = ((), (), s32[]{:S(2)}) async-start(), calls=%async_computation.24 | async-start | bytes 2949120
  508.6 289.6 %reduce-scatter.46.cloned.1.call-start = ((), (), s32[]{:S(2)}) async-start(), calls=%async_computation.26 | async-start | bytes 2949120
  510.6 385.5 %reduce-scatter.32.cloned.1.call-start = ((), (), s32[]{:S(2)}) async-start(), calls=%async_computation.19 | async-start | bytes 11796480 | tf_op jit(solution)/shard_map/reduce_scatter | solution.py:311
  517.9 476.1 %reduce-scatter.36.cloned.1.call-start = ((), (), s32[]{:S(2)}) async-start(), calls=%async_computation.21 | async-start | bytes 11796480 | tf_op jit(solution)/shard_map/reduce_scatter | solution.py:313
  526.0 565.9 %reduce-scatter.38.cloned.1.call-start = ((), (), s32[]{:S(2)}) async-start(), calls=%async_computation.22 | async-start | bytes 11796480 | tf_op jit(solution)/shard_map/reduce_scatter | solution.py:328
  532.9 656.9 %reduce-scatter.34.cloned.1.call-start = ((), (), s32[]{:S(2)}) async-start(), calls=%async_computation.20 | async-start | bytes 11796480 | tf_op jit(solution)/shard_map/reduce_scatter | solution.py:326
  538.9 705.3 %all-reduce.26.cloned.1.call-start = ((), (), s32[]{:S(2)}) async-start(), calls=%async_computation.33 | async-start | bytes 180224
  548.4 723.2 %reduce-scatter.56.cloned.1.call-start = ((), (), s32[]{:S(2)}) async-start(), calls=%async_computation.31 | async-start | bytes 491520
  549.5 1041.6 %all-reduce.24.cloned.1.call-start = ((), (), s32[]{:S(2)}) async-start(), calls=%async_computation.32 | async-start | bytes 31457280 | tf_op jit(solution)/shard_map/psum | solution.py:334
  (109 other events, 1417.8 us)
Sparse Core Ops, SparseCore 0:
  9.8 40.0 all-gather.9
  51.8 37.3 all-gather.11
  91.0 37.3 all-gather.13
  130.1 37.3 all-gather.15
  169.1 96.1 all-gather.17
  267.1 96.1 all-gather.19
  477.4 37.3 reduce-scatter.47
  517.9 37.3 reduce-scatter.39
  558.3 37.3 reduce-scatter.43
  598.6 37.3 reduce-scatter.51
  639.1 37.3 reduce-scatter.53
  679.4 37.3 reduce-scatter.49
  720.5 37.3 reduce-scatter.41
  760.8 37.3 reduce-scatter.45
  801.2 94.8 reduce-scatter.31
  899.1 94.8 reduce-scatter.35
  997.0 94.8 reduce-scatter.37
  1094.8 94.8 reduce-scatter.33
  1195.7 48.4 all-reduce.25
  1246.9 24.6 reduce-scatter.55
  1276.2 314.8 all-reduce.23
where the time goes:
time: 1630 us; the launch traced here: 1620 us
  waiting for transfers between devices  1260 us (77%)
  matrix products  130 us (8%)
  local copies, waits for them, and re-layouts  81.8 us (5%)
  other arithmetic  69.1 us (4%)
  blocking collectives  60.5 us (4%)
  between operations  17.4 us (1%)
    unnamed x31, waiting for transfers between devices  295 us
    psum x1, waiting for transfers between devices, shards(): lax.psum((shares[0], shares[1], shares[2], shares[3], shares[4], shares[5...  282 us
    reduce_scatter x1, waiting for transfers between devices, shards(): lax.psum_scatter(cross_grads[9], 'dp', scatter_dimension=0, tiled=True)  97.9 us
    reduce_scatter x1, waiting for transfers between devices, shards(): lax.psum_scatter(segment_grads[11], 'dp', scatter_dimension=0, tiled=True)  97.9 us
    reduce_scatter x1, waiting for transfers between devices, shards(): lax.psum_scatter(cross_grads[11], 'dp', scatter_dimension=0, tiled=True)  97.9 us
    reduce_scatter x1, waiting for transfers between devices, shards(): lax.psum_scatter(segment_grads[9], 'dp', scatter_dimension=0, tiled=True)  95.7 us
    all_gather x1, waiting for transfers between devices, shards(): lax.all_gather(inner_weight, 'dp', axis=1, tiled=True)  95.4 us
    all_gather x1, waiting for transfers between devices, shards(): lax.all_gather(outer_weight, 'dp', axis=1, tiled=True)  72.1 us
  transfers between devices with their start and end apart: 21, of which 20 were waited for; matrix products, arithmetic and copies ran while one was open for 9% of the time, Pallas kernels for 0%

commit v1 on v0

--- a/solution.py
+++ b/solution.py
@@ -7,6 +7,27 @@
 HEAD_DIM = 64
 SEG_LEN = 128
 epsilon = 1e-05
+
+
+def joined_along(pieces, dim):
+    pieces = jnp.moveaxis(pieces, 0, dim)
+    shape = pieces.shape
+    return pieces.reshape(*shape[:dim], shape[dim] * shape[dim + 1], *shape[dim + 2 :])
+
+
+def collected_by_bits(shard, axis):
+    devices, index = (lax.axis_size(axis), lax.axis_index(axis))
+    blocks, distance = (shard[None], 1)
+    while distance < devices:
+        other = lax.ppermute(blocks, axis, [(i, i ^ distance) for i in range(devices)])
+        low = index & distance == 0
+        blocks = jnp.concatenate([jnp.where(low, blocks, other), jnp.where(low, other, blocks)])
+        distance *= 2
+    return blocks
+
+
+def doubled_up(x, axis, dim):
+    return joined_along(collected_by_bits(x, axis), dim)
 
 
 def normalize(values, gain, shift):
@@ -241,7 +262,7 @@
         lax.all_gather(key_weight, "dp", axis=1, tiled=True),
         lax.all_gather(value_weight, "dp", axis=1, tiled=True),
         lax.all_gather(out_weight, "dp", axis=1, tiled=True),
-        lax.all_gather(inner_weight, "dp", axis=1, tiled=True),
+        doubled_up(inner_weight, "dp", 1),
         lax.all_gather(outer_weight, "dp", axis=1, tiled=True),
     )
     stacked = (

time: 1630 us -> 1540 us (0.945)
  waiting for transfers between devices: 1260 us -> 1150 us
    all_gather x1 -> x0, waiting for transfers between devices: 95.4 us -> none  [shards(): lax.all_gather(inner_weight, 'dp', axis=1, tiled=True)]
    ppermute x0 -> x2, waiting for transfers between devices: none -> 74.3 us  [collected_by_bits(): lax.ppermute(blocks, axis, [(i, i ^ distance) for i in range(devices)])]
    unnamed x31 -> x30, waiting for transfers between devices: 295 us -> 239 us
    all_gather x1, waiting for transfers between devices: 36 us -> 0.01 us  [shards(): lax.all_gather(query_weight, 'dp', axis=1, tiled=True)]
    all_gather x1, waiting for transfers between devices: 17.8 us -> 53.2 us  [shards(): lax.all_gather(value_weight, 'dp', axis=1, tiled=True)]
    all_gather x1, waiting for transfers between devices: 36.8 us -> 5.01 us  [shards(): lax.all_gather(key_weight, 'dp', axis=1, tiled=True)]
    unnamed x261 -> x251, local copies, waits for them, and re-layouts: 68.9 us -> 66.7 us
  transfers between devices with their start and end apart: 21 -> 22, of which waited for: 20 -> 17; matrix products, arithmetic and copies ran while one was open for 9% -> 15% of each run, Pallas kernels for 0% -> 0%
where the time goes in v1:
time: 1540 us
  waiting for transfers between devices  1150 us (75%)
  matrix products  142 us (9%)
  local copies, waits for them, and re-layouts  91.9 us (6%)
  other arithmetic  71.8 us (5%)
  blocking collectives  60 us (4%)
  between operations  17.4 us (1%)
    psum x1, waiting for transfers between devices, shards(): lax.psum((shares[0], shares[1], shares[2], shares[3], shares[4], shares[5...  282 us
    unnamed x30, waiting for transfers between devices  239 us
    reduce_scatter x1, waiting for transfers between devices, shards(): lax.psum_scatter(segment_grads[9], 'dp', scatter_dimension=0, tiled=True)  97.9 us
    reduce_scatter x1, waiting for transfers between devices, shards(): lax.psum_scatter(cross_grads[9], 'dp', scatter_dimension=0, tiled=True)  97.9 us
    reduce_scatter x1, waiting for transfers between devices, shards(): lax.psum_scatter(cross_grads[11], 'dp', scatter_dimension=0, tiled=True)  97.9 us
    reduce_scatter x1, waiting for transfers between devices, shards(): lax.psum_scatter(segment_grads[11], 'dp', scatter_dimension=0, tiled=True)  95.7 us
    ppermute x2, waiting for transfers between devices, collected_by_bits(): lax.ppermute(blocks, axis, [(i, i ^ distance) for i in range(devices)])  74.3 us
    unnamed x251, local copies, waits for them, and re-layouts  66.7 us
  transfers between devices with their start and end apart: 22, of which 17 were waited for; matrix products, arithmetic and copies ran while one was open for 15% of the time, Pallas kernels for 0%

profile of v1, /device:TPU:0, one launch (start us, length us, event | category | flops | bytes accessed | tf_op | source)
XLA Modules:
  0.0 1535.9 jit_solution(6975883399805418757)
XLA Ops:
  13.2 74.3 %collective-permute-done = bf16[1,2,192,3072]{3,2,1,0:T(8,128)(2,1)} collective-permute-done((bf16[1,2,192,3072]{3,2,1,0:T(8,128)(2,1)S(1)}, bf16[1,2,192,3072]{3,2,1,0:T(8,128)(2,1)}, u32[]{:S(2)}, u32[]{:S(2)}) %collective-permute-start) | collective-permute-done | bytes 2359328 | tf_op jit(solution)/shard_map/ppermute | solution.py:22
  95.4 14.3 all-gather.1
  129.6 53.2 %all-gather.9.cloned.1.call-done = bf16[2,768,768]{2,1,0:T(8,128)(2,1)} async-done(((bf16[2,192,768]{2,1,0:T(8,128)(2,1)}), bf16[2,768,768]{2,1,0:T(8,128)(2,1)}) %all-gather.9.cloned.1.call-update) | async-done | bytes 2359312 | tf_op jit(solution)/shard_map/all_gather | solution.py:263
  196.1 44.6 %all-gather.15.cloned.1.call-done = bf16[2,768,768]{2,1,0:T(8,128)(2,1)} async-done(((bf16[2,192,768]{2,1,0:T(8,128)(2,1)}), bf16[2,768,768]{2,1,0:T(8,128)(2,1)}) %all-gather.15.cloned.1.call-update) | async-done | bytes 2359312 | tf_op jit(solution)/shard_map/all_gather | solution.py:264
  253.8 7.8 fusion.28
  264.1 15.5 %multiply_convert_fusion = (bf16[4,128,3072]{2,1,0:T(8,128)(2,1)}, f32[4,128,3072]{2,1,0:T(8,128)}) fusion(f32[4,128,3072]{2,1,0:T(8,128)S(1)} %get-tuple-element.189, f32[3072]{0:T(1024)S(1)} %bitcast.350, u8[128,3072]{1,0:T(8,128)(4,1)S(1)} %get-tuple-element.73, u8[128,3072]{1,0:T(8,128)(4,1)S(1)} %get-tuple-element.72), kind=kLoop, calls=%fused_computation.20 | loop fusion | flops 111673344 | bytes 16527360 | tf_op jit(solution)/shard_map/convert_element_type | solution.py:114
  279.7 59.3 %all-gather.17.cloned.1.call-done = bf16[2,3072,768]{2,1,0:T(8,128)(2,1)} async-done(((bf16[2,768,768]{2,1,0:T(8,128)(2,1)}), bf16[2,3072,768]{2,1,0:T(8,128)(2,1)}) %all-gather.17.cloned.1.call-update) | async-done | bytes 9437200 | tf_op jit(solution)/shard_map/all_gather | solution.py:266
  348.2 14.5 all-gather.2
  429.3 9.9 convert_reduce_fusion
  486.1 8.2 convolution_bitcast_fusion
  501.7 7.3 convolution_bitcast_fusion.1
  532.4 24.3 %reduce-scatter.52.cloned.1.call-done = f32[192,768]{1,0:T(8,128)} async-done(((f32[768,768]{1,0:T(8,128)}), f32[192,768]{1,0:T(8,128)}) %reduce-scatter.52.cloned.1.call-update) | async-done | bytes 589840
  559.0 38.1 %reduce-scatter.48.cloned.1.call-done = f32[192,768]{1,0:T(8,128)} async-done(((f32[768,768]{1,0:T(8,128)}), f32[192,768]{1,0:T(8,128)}) %reduce-scatter.48.cloned.1.call-update) | async-done | bytes 589840
  599.3 38.8 %reduce-scatter.42.cloned.1.call-done = f32[192,768]{1,0:T(8,128)} async-done(((f32[768,768]{1,0:T(8,128)}), f32[192,768]{1,0:T(8,128)}) %reduce-scatter.42.cloned.1.call-update) | async-done | bytes 589840
  640.3 38.1 %reduce-scatter.40.cloned.1.call-done = f32[192,768]{1,0:T(8,128)} async-done(((f32[768,768]{1,0:T(8,128)}), f32[192,768]{1,0:T(8,128)}) %reduce-scatter.40.cloned.1.call-update) | async-done | bytes 589840
  680.6 38.2 %reduce-scatter.44.cloned.1.call-done = f32[192,768]{1,0:T(8,128)} async-done(((f32[768,768]{1,0:T(8,128)}), f32[192,768]{1,0:T(8,128)}) %reduce-scatter.44.cloned.1.call-update) | async-done | bytes 589840
  721.0 95.7 %reduce-scatter.36.cloned.1.call-done = f32[768,768]{1,0:T(8,128)} async-done(((f32[3072,768]{1,0:T(8,128)}), f32[768,768]{1,0:T(8,128)}) %reduce-scatter.36.cloned.1.call-update) | async-done | bytes 2359312 | tf_op jit(solution)/shard_map/reduce_scatter | solution.py:334
  816.7 97.9 %reduce-scatter.38.cloned.1.call-done = f32[768,768]{1,0:T(8,128)} async-done(((f32[3072,768]{1,0:T(8,128)}), f32[768,768]{1,0:T(8,128)}) %reduce-scatter.38.cloned.1.call-update) | async-done | bytes 2359312 | tf_op jit(solution)/shard_map/reduce_scatter | solution.py:349
  914.6 97.9 %reduce-scatter.32.cloned.1.call-done = f32[192,3072]{1,0:T(8,128)} async-done(((f32[768,3072]{1,0:T(8,128)}), f32[192,3072]{1,0:T(8,128)}) %reduce-scatter.32.cloned.1.call-update) | async-done | bytes 2359312 | tf_op jit(solution)/shard_map/reduce_scatter | solution.py:332
  1012.5 97.9 %reduce-scatter.34.cloned.1.call-done = f32[192,3072]{1,0:T(8,128)} async-done(((f32[768,3072]{1,0:T(8,128)}), f32[192,3072]{1,0:T(8,128)}) %reduce-scatter.34.cloned.1.call-update) | async-done | bytes 2359312 | tf_op jit(solution)/shard_map/reduce_scatter | solution.py:347
  1120.1 44.5 %all-reduce.26.cloned.1.call-done = (f32[768]{0:T(1024)}, f32[768]{0:T(1024)}, f32[768]{0:T(1024)}, f32[768]{0:T(1024)}, f32[768]{0:T(1024)}, /*index=5*/f32[768...) async-done(((f32[768]{0:T(1024)}, f32[768]{0:T(1024)}, ...) | async-done | bytes 73744
  1178.2 14.0 reduce-scatter.56.cloned.1.call-done
  1193.1 31.2 %all-reduce.18 = (f32[1,192]{1,0:T(1,128)S(1)}, f32[1,192]{1,0:T(1,128)S(1)}, f32[1,192]{1,0:T(1,128)S(1)}, f32[1,192]{1,0:T(1,128)S(1)}, f32[1,192]{1,0:T(1,128...) all-reduce(f32[1,192]{1,0:T(1,128)S(1)} %bitcast.354, ...), channel_id=1, replica_groups=mesh['dp'=4,'seg'=8] {'seg'}, use_global_device_ids=true, to_apply=%region_31.32 | all-reduce | flops 10752 | bytes 86016 | tf_op jit(solution)/shard_map/psum | solution.py:355
  1229.5 282.0 %all-reduce.24.cloned.1.call-done = (f32[1,192,768]{1,2,0:T(8,128)}, f32[1,192,768]{1,2,0:T(8,128)}, f32[1,192,768]{1,2,0:T(8,128)}, f32[1,192,768]{1,2,0:T(8,12...) async-done(((f32[1,192,768]{1,2,0:T(8,128)}, ...) | async-done | bytes 14155792 | tf_op jit(solution)/shard_map/psum | solution.py:355
  (454 shorter events, 271.3 us)
Async XLA Ops:
  7.2 107.0 %all-gather.11.cloned.1.call-start = ((), (), s32[]{:S(2)}) async-start(), calls=%async_computation.14 | async-start | bytes 2949120 | tf_op jit(solution)/shard_map/all_gather | solution.py:261
  7.9 116.5 %all-gather.13.cloned.1.call-start = ((), (), s32[]{:S(2)}) async-start(), calls=%async_computation.15 | async-start | bytes 2949120 | tf_op jit(solution)/shard_map/all_gather | solution.py:262
  8.7 174.1 %all-gather.9.cloned.1.call-start = ((), (), s32[]{:S(2)}) async-start(), calls=%async_computation.13 | async-start | bytes 2949120 | tf_op jit(solution)/shard_map/all_gather | solution.py:263
  9.4 231.3 %all-gather.15.cloned.1.call-start = ((), (), s32[]{:S(2)}) async-start(), calls=%async_computation.16 | async-start | bytes 2949120 | tf_op jit(solution)/shard_map/all_gather | solution.py:264
  10.0 328.9 %all-gather.17.cloned.1.call-start = ((), (), s32[]{:S(2)}) async-start(), calls=%async_computation.17 | async-start | bytes 11796480 | tf_op jit(solution)/shard_map/all_gather | solution.py:266
  10.1 77.4 %collective-permute-start = (bf16[1,2,192,3072]{3,2,1,0:T(8,128)(2,1)S(1)}, bf16[1,2,192,3072]{3,2,1,0:T(8,128)(2,1)}, u32[]{:S(2)}, u32[]{:S(2)}) collective-permute-start(bf16[1,2,192,3072]{3,2,1,0:T(8,128)(2,1)S(1)} %bitcast.336), channel_id=1, source_target_pairs={{0,8},{8,0},{16,24},{24,16},{1,9},{9,1},{17,25},{25,17},{2,10},{10... | collective-permute-start | bytes 7077896 | tf_op jit(solution)/shard_map/ppermute | solution.py:22
  13.1 512.6 %reduce-scatter.54.cloned.1.call-start = ((), (), s32[]{:S(2)}) async-start(), calls=%async_computation.29 | async-start | bytes 2949120
  93.1 151.4 %collective-permute-start.1 = (bf16[2,2,192,3072]{3,2,1,0:T(8,128)(2,1)}, bf16[2,2,192,3072]{3,2,1,0:T(8,128)(2,1)}, u32[]{:S(2)}, u32[]{:S(2)}) collective-permute-start(bf16[2,2,192,3072]{3,2,1,0:T(8,128)(2,1)} %pad_maximum_fusion), channel_id=1, source_target_pairs={{0,16},{8,24},{16,0},{24,8},{1,17},{9,25},{17,1},{25,9},{2,18},{10... | collective-permute-start | bytes 14155784 | tf_op jit(solution)/shard_map/ppermute | solution.py:22
  111.6 227.3 %copy-start.78 = (f32[768]{0:T(1024)}, f32[768]{0:T(1024)S(1)}, u32[]{:S(2)}) copy-start(f32[768]{0:T(1024)S(1)} %get-tuple-element.91) | copy-start | bytes 9220
  112.9 233.0 %copy-start.55 = (f32[768]{0:T(1024)}, f32[768]{0:T(1024)S(1)}, u32[]{:S(2)}) copy-start(f32[768]{0:T(1024)S(1)} %get-tuple-element.215) | copy-start | bytes 9220
  397.8 130.1 %reduce-scatter.50.cloned.1.call-start = ((), (), s32[]{:S(2)}) async-start(), calls=%async_computation.27 | async-start | bytes 2949120
  407.3 122.9 %reduce-scatter.46.cloned.1.call-start = ((), (), s32[]{:S(2)}) async-start(), calls=%async_computation.25 | async-start | bytes 2949120
  426.3 130.5 %reduce-scatter.52.cloned.1.call-start = ((), (), s32[]{:S(2)}) async-start(), calls=%async_computation.28 | async-start | bytes 2949120
  447.7 149.4 %reduce-scatter.48.cloned.1.call-start = ((), (), s32[]{:S(2)}) async-start(), calls=%async_computation.26 | async-start | bytes 2949120
  462.1 176.0 %reduce-scatter.42.cloned.1.call-start = ((), (), s32[]{:S(2)}) async-start(), calls=%async_computation.23 | async-start | bytes 2949120
  464.7 213.6 %reduce-scatter.40.cloned.1.call-start = ((), (), s32[]{:S(2)}) async-start(), calls=%async_computation.22 | async-start | bytes 2949120
  476.1 242.7 %reduce-scatter.44.cloned.1.call-start = ((), (), s32[]{:S(2)}) async-start(), calls=%async_computation.24 | async-start | bytes 2949120
  484.8 331.9 %reduce-scatter.36.cloned.1.call-start = ((), (), s32[]{:S(2)}) async-start(), calls=%async_computation.20 | async-start | bytes 11796480 | tf_op jit(solution)/shard_map/reduce_scatter | solution.py:334
  494.3 420.3 %reduce-scatter.38.cloned.1.call-start = ((), (), s32[]{:S(2)}) async-start(), calls=%async_computation.21 | async-start | bytes 11796480 | tf_op jit(solution)/shard_map/reduce_scatter | solution.py:349
  501.1 511.4 %reduce-scatter.32.cloned.1.call-start = ((), (), s32[]{:S(2)}) async-start(), calls=%async_computation.18 | async-start | bytes 11796480 | tf_op jit(solution)/shard_map/reduce_scatter | solution.py:332
  509.0 601.3 %reduce-scatter.34.cloned.1.call-start = ((), (), s32[]{:S(2)}) async-start(), calls=%async_computation.19 | async-start | bytes 11796480 | tf_op jit(solution)/shard_map/reduce_scatter | solution.py:347
  515.1 649.5 %all-reduce.26.cloned.1.call-start = ((), (), s32[]{:S(2)}) async-start(), calls=%async_computation.32 | async-start | bytes 180224
  524.6 667.6 %reduce-scatter.56.cloned.1.call-start = ((), (), s32[]{:S(2)}) async-start(), calls=%async_computation.30 | async-start | bytes 491520
  525.6 985.9 %all-reduce.24.cloned.1.call-start = ((), (), s32[]{:S(2)}) async-start(), calls=%async_computation.31 | async-start | bytes 31457280 | tf_op jit(solution)/shard_map/psum | solution.py:355
  (105 other events, 1212.7 us)
Sparse Core Ops, SparseCore 0:
  9.8 58.9 all-gather.10
  70.7 53.6 all-gather.12
  126.2 56.4 all-gather.8
  184.5 56.1 all-gather.14
  242.4 96.5 all-gather.16
  398.0 37.3 reduce-scatter.53
  438.4 37.3 reduce-scatter.49
  478.8 37.3 reduce-scatter.45
  519.3 37.3 reduce-scatter.51
  559.6 37.3 reduce-scatter.47
  600.7 37.3 reduce-scatter.41
  641.0 37.3 reduce-scatter.39
  681.4 37.3 reduce-scatter.43
  721.8 94.8 reduce-scatter.35
  819.7 94.8 reduce-scatter.37
  917.5 94.8 reduce-scatter.31
  1015.4 94.8 reduce-scatter.33
  1116.1 48.4 all-reduce.25
  1167.4 24.6 reduce-scatter.55
  1196.6 314.9 all-reduce.23
